TPU v7x, 32 devices: a whole 2x2x4 slice. The times are simulated.
32 devices in a mesh: row: 8 (over y, x, core), col: 4 (over z).
Axes of the slice: x: 2, y: 2, z: 4, core: 2. Of those that a mesh axis runs over, the one named last changes fastest.
Arguments:
- earlier_blocks: bfloat16 [32, 8, 128, 128], P('row', 'col'), may hold values from -0.5 to 0.5
- later_blocks: bfloat16 [8, 32, 128, 128], P('row', 'col'), may hold values from -6 to 6
- earlier_pattern: int32 [32, 8], P('row', 'col'), may hold values from 0 to 1, as said below
- later_pattern: int32 [8, 32], P('row', 'col'), may hold values from 0 to 1, as said below
- triples: int32 [32, 32, 48], P('row', 'col'), may hold values from 0 to 7
Outputs:
- composed: float32 [32, 32, 128, 128], P('row', 'col')
Inputs may be any that keep to these rules, and one draw needn't show every extreme that they name: `earlier_pattern`: in each aligned share of 4 x 2 entries held by one device, at most 4 entries are 1, and exactly 4 in some share. `later_pattern`: in each aligned share of 1 x 8 entries held by one device, at most 4 entries are 1, and exactly 4 in some share.
All inputs are finite; a program needn't handle non-finite values.
Results may differ from a plain program's by a relative error of at most 0.0003.
Values may be sent and summed in bfloat16 or wider, within the bound.
A program may use at most 256 MiB of HBM per device.

v0:
```python
import functools

import jax
import jax.numpy as jnp
from jax import lax
from jax.experimental import pallas as pl
from jax.experimental.pallas import tpu as pltpu
from jax.sharding import PartitionSpec as P

MESH = pl.DeviceIdType.MESH
LANES = 128


def slot_positions(pattern, count_a, count_b, capacity):
    slots = []
    for slot in range(capacity):
        at_a, at_b, found = jnp.int32(0), jnp.int32(0), jnp.int32(0)
        rank = jnp.int32(0)
        for a in range(count_a):
            for b in range(count_b):
                live = pattern(a, b)
                hit = jnp.logical_and(live == 1, rank == slot)
                at_a = jnp.where(hit, a, at_a)
                at_b = jnp.where(hit, b, at_b)
                found = jnp.where(hit, 1, found)
                rank = rank + live
        slots.append((at_a, at_b, found))
    return slots


def pack(blocks_ref, pattern, packed_ref, meta_ref):
    lane = lax.broadcasted_iota(jnp.int32, meta_ref.shape, 1)
    meta = jnp.zeros(meta_ref.shape, jnp.int32)
    slots = slot_positions(pattern, *blocks_ref.shape[:2], packed_ref.shape[0])
    for slot, (at_a, at_b, found) in enumerate(slots):
        packed_ref[slot] = blocks_ref[at_a, at_b]
        for part, value in enumerate((at_a, at_b, found)):
            meta = jnp.where(lane == 3 * slot + part, value, meta)
    meta_ref[...] = meta


def gather_kernel(
    n_row, n_col, middle,
    e_hbm, l_hbm, ep_ref, lp_ref, t_ref,
    eg_ref, lg_ref, em_ref, lm_ref, cnt_ref,
    e_ref, l_ref, pe_ref, pl_ref, me_ref, ml_ref,
    send_e, recv_e, send_l, recv_l, send_f, recv_f, local_sem, fetch_sem,
):
    row, col = lax.axis_index("row"), lax.axis_index("col")
    partner = row + 1 - 2 * lax.rem(row, 2)
    row_steps = range(1, n_row // 2)
    row_to = [(lax.rem(row + 2 * d, n_row), col) for d in row_steps]
    slots_e = pe_ref.shape[0]
    has_right = col < n_col - 1
    has_left = col > 0

    barrier = pltpu.get_barrier_semaphore()
    others = row_to + [(partner, col)]
    for other in others:
        pl.semaphore_signal(barrier, inc=1, device_id=other, device_id_type=MESH)
    for there, step in ((has_right, 1), (has_left, -1)):
        @pl.when(there)
        def _():
            pl.semaphore_signal(
                barrier, inc=1, device_id=(row, col + step), device_id_type=MESH
            )
    fetch_e = pltpu.make_async_copy(e_hbm, e_ref, fetch_sem.at[0])
    fetch_l = pltpu.make_async_copy(l_hbm, l_ref, fetch_sem.at[1])
    fetch_e.start()
    fetch_l.start()
    fetch_e.wait()
    pack(e_ref, lambda a, b: ep_ref[b, a], pe_ref, me_ref)
    fetch_l.wait()
    pack(l_ref, lambda a, b: lp_ref[a, b], pl_ref, ml_ref)
    ends = has_right.astype(jnp.int32) + has_left.astype(jnp.int32)
    pl.semaphore_wait(barrier, len(others) + ends)

    def remote(src, dst, send, recv, device):
        return pltpu.make_async_remote_copy(
            src_ref=src, dst_ref=dst, send_sem=send, recv_sem=recv,
            device_id=device, device_id_type=MESH,
        )

    def pair(srcs, dsts, where, send, recv, d, device):
        return [
            remote(srcs[n], dsts[n].at[where], send.at[n, d], recv.at[n, d], device)
            for n in range(2)
        ]

    def along(way, hop, chunk):
        step = 1 - 2 * way
        source = col - step * hop
        if chunk == slots_e:
            src = me_ref if hop == 0 else em_ref.at[source]
            dst = em_ref.at[source]
        else:
            src = pe_ref.at[chunk] if hop == 0 else eg_ref.at[source, chunk]
            dst = eg_ref.at[source, chunk]
        return remote(
            src, dst, send_e.at[way, hop, chunk], recv_e.at[way, hop, chunk],
            (row, col + step),
        )

    def sends(way, hop):
        if way == 0:
            return jnp.logical_and(has_right, col >= hop)
        return jnp.logical_and(has_left, col + hop < n_col)

    def receives(way, hop):
        return col >= hop + 1 if way == 0 else col + hop + 1 < n_col

    hops = range(n_col - 1)
    chunks = range(slots_e + 1)
    for chunk in chunks:
        for way in range(2):
            @pl.when(sends(way, 0))
            def _():
                along(way, 0, chunk).start()

    later_out, later_own = (lg_ref, lm_ref), (pl_ref, ml_ref)
    to_rows = [
        pair(later_own, later_out, row, send_l, recv_l, d, device)
        for d, device in zip(row_steps, row_to)
    ]
    forwards = [pair(later_own, later_out, row, send_f, recv_f, 0, (partner, col))]
    for group in to_rows + forwards:
        for copy in group:
            copy.start()
    locals_ = [
        pltpu.make_async_copy(src, dst, local_sem.at[n])
        for n, (src, dst) in enumerate((
            (pl_ref, lg_ref.at[row]), (ml_ref, lm_ref.at[row]),
            (pe_ref, eg_ref.at[col]), (me_ref, em_ref.at[col]),
        ))
    ]
    for copy in locals_:
        copy.start()

    rows, cols, listed = t_ref.shape
    lane = lax.broadcasted_iota(jnp.int32, (cols, LANES), 1)
    for i in range(rows):
        numbers = t_ref[i]
        counts = jnp.zeros((cols, LANES), jnp.float32)
        for k in range(middle):
            hits = jnp.sum(jnp.where(numbers == k, 1.0, 0.0), axis=1, keepdims=True)
            counts = jnp.where(lane == k, hits, counts)
        cnt_ref[pl.ds(i * cols, cols), :] = counts

    def land(hop):
        for chunk in chunks:
            for way in range(2):
                @pl.when(receives(way, hop))
                def _():
                    along(way, hop, chunk).wait_recv()
                if hop + 1 < n_col - 1:
                    @pl.when(sends(way, hop + 1))
                    def _():
                        along(way, hop + 1, chunk).start()

    for hop in hops[:-1]:
        land(hop)
    for d, group in zip(row_steps, to_rows):
        for copy in group:
            copy.wait_recv()
        source = lax.rem(row + n_row - 2 * d, n_row)
        onward = pair(
            (lg_ref.at[source], lm_ref.at[source]), later_out, source,
            send_f, recv_f, d, (partner, col),
        )
        for copy in onward:
            copy.start()
        forwards.append(onward)
    for hop in hops[-1:]:
        land(hop)
    for group in forwards:
        for copy in group:
            copy.wait_recv()
    for group in to_rows + forwards:
        for copy in group:
            copy.wait_send()
    for hop in hops:
        for way in range(2):
            @pl.when(sends(way, hop))
            def _():
                for chunk in chunks:
                    along(way, hop, chunk).wait_send()
    for copy in locals_:
        copy.wait()


def compose_kernel(early_ka, late_kb, eg_ref, lg_ref, em_ref, lm_ref, cnt_ref, out_ref):
    n_col, slots_e = eg_ref.shape[:2]
    slots_l = lg_ref.shape[1]
    rows, cols = out_ref.shape[:2]
    out_ref[...] = jnp.zeros_like(out_ref)
    for c in range(n_col):
        for s in range(slots_e):
            i = em_ref[c, 0, 3 * s]
            k = c * early_ka + em_ref[c, 0, 3 * s + 1]
            live_e = em_ref[c, 0, 3 * s + 2]
            source = k // late_kb if late_kb > 1 else k
            later = jnp.concatenate([lg_ref[source, u] for u in range(slots_l)], axis=1)
            product = jnp.dot(eg_ref[c, s], later, preferred_element_type=jnp.float32)
            for u in range(slots_l):
                k_l = source * late_kb + lm_ref[source, 0, 3 * u]
                j = lm_ref[source, 0, 3 * u + 1]
                live = jnp.logical_and(live_e * lm_ref[source, 0, 3 * u + 2] == 1, k_l == k)
                weight = jnp.where(live, cnt_ref[i * cols + j, k], 0.0)
                out_ref[i, j] += weight * product[:, u * LANES:(u + 1) * LANES]


def on_device(n_row, n_col, earlier_blocks, later_blocks, earlier_pattern, later_pattern, triples):
    rows, early_ka, side, _ = earlier_blocks.shape
    late_kb, cols = later_blocks.shape[:2]
    slots_e = max(1, rows * early_ka // 2)
    slots_l = max(1, late_kb * cols // 2)
    middle = n_row * late_kb
    vmem = pl.BlockSpec(memory_space=pltpu.VMEM)
    smem = pl.BlockSpec(memory_space=pltpu.SMEM)
    hbm = pl.BlockSpec(memory_space=pl.ANY)
    block = jnp.bfloat16
    eg, lg, em, lm, counts = pl.pallas_call(
        functools.partial(gather_kernel, n_row, n_col, middle),
        out_shape=(
            jax.ShapeDtypeStruct((n_col, slots_e, side, side), block),
            jax.ShapeDtypeStruct((n_row, slots_l, side, side), block),
            jax.ShapeDtypeStruct((n_col, 1, LANES), jnp.int32),
            jax.ShapeDtypeStruct((n_row, 1, LANES), jnp.int32),
            jax.ShapeDtypeStruct((rows * cols, LANES), jnp.float32),
        ),
        in_specs=[hbm, hbm, smem, smem, vmem],
        out_specs=(hbm, hbm, hbm, hbm, vmem),
        scratch_shapes=[
            pltpu.VMEM(earlier_blocks.shape, block),
            pltpu.VMEM(later_blocks.shape, block),
            pltpu.VMEM((slots_e, side, side), block),
            pltpu.VMEM((slots_l, side, side), block),
            pltpu.VMEM((1, LANES), jnp.int32),
            pltpu.VMEM((1, LANES), jnp.int32),
            pltpu.SemaphoreType.DMA((2, n_col, slots_e + 1)),
            pltpu.SemaphoreType.DMA((2, n_col, slots_e + 1)),
            pltpu.SemaphoreType.DMA((2, n_row)),
            pltpu.SemaphoreType.DMA((2, n_row)),
            pltpu.SemaphoreType.DMA((2, n_row)),
            pltpu.SemaphoreType.DMA((2, n_row)),
            pltpu.SemaphoreType.DMA((4,)),
            pltpu.SemaphoreType.DMA((2,)),
        ],
        compiler_params=pltpu.CompilerParams(collective_id=0, has_side_effects=True),
        name="gather_live",
    )(earlier_blocks, later_blocks, earlier_pattern.T, later_pattern, triples)
    return pl.pallas_call(
        functools.partial(compose_kernel, early_ka, late_kb),
        out_shape=jax.ShapeDtypeStruct((rows, cols, side, side), jnp.float32),
        in_specs=[vmem, vmem, smem, smem, smem],
        out_specs=vmem,
        name="compose",
    )(eg, lg, em, lm, counts)


def solution(mesh):
    return jax.shard_map(
        functools.partial(on_device, mesh.shape["row"], mesh.shape["col"]),
        mesh=mesh,
        in_specs=(
            P("row", "col", None, None),
            P("row", "col", None, None),
            P("row", "col"),
            P("row", "col"),
            P("row", "col", None),
        ),
        out_specs=P("row", "col", None, None),
        check_vma=False,
    )
```

profile of v0, /device:TPU:0, one launch (start us, length us, event | category | flops | bytes accessed | tf_op | source)
XLA Modules:
  0.0 22.7 jit_solution(1162338825584289277)
XLA Ops:
  0.0 19.1 %gather_live.1 = (bf16[4,4,128,128]{3,2,1,0:T(8,128)(2,1)}, bf16[8,4,128,128]{3,2,1,0:T(8,128)(2,1)}, s32[4,1,128]{2,1,0:T(1,128)}, s32[8,1,128]{2,1,0:T(1,128)}, f32[32,128]{1,0:T(8,128)}) custom-call(bf16[4,2,128,128]{3,2,1,0:T(8,128)(2,1)} %e_hbm.1, bf16[1,8,128,128]{3,2,1,0:T(8,128)(2,1)} %l_hbm.1, s32[2,4]{1,0:T(2,128)} %bitcast.1, s32[1,8]{1,0:T(1,128)} %lp_ref.1, ...), custom_call_target="tpu_custom_call" | custom-call | tf_op jit(solution)/shard_map/gather_live/pallas_call | solution.py:222
  19.1 3.6 %compose.1 = f32[4,8,128,128]{3,2,1,0:T(8,128)} custom-call(bf16[4,4,128,128]{3,2,1,0:T(8,128)(2,1)} %get-tuple-element.10.eg_ref, bf16[8,4,128,128]{3,2,1,0:T(8,128)(2,1)} %get-tuple-element.11.lg_ref, s32[4,1,128]{2,1,0:T(1,128)} %get-tuple-element.12.em_ref, s32[8,1,128]{2,1,0:T(1,128)} %get-tuple-element.13.lm_ref, f32[32,128]{1,0:T(8,128)} %get-tuple-element.14.cnt_ref), custom_call_target="tpu_custom_call" | custom-call | tf_op jit(solution)/shard_map/compose/pallas_call | solution.py:252
where the time goes:
time: 23 us; the launch traced here: 22.7 us
  Pallas kernels  22.7 us (99%)
    pallas_call x1, Pallas kernels, on_device(): pl.pallas_call(functools.partial(gather_kernel, n_row, n_col, middle), ou...  19.1 us
    pallas_call x1, Pallas kernels, on_device(): pl.pallas_call(functools.partial(compose_kernel, early_ka, late_kb), out_...  3.56 us

commit v1 on v0

v1 whole, which is shorter than its diff:
```python
import functools

import jax
import jax.numpy as jnp
from jax import lax
from jax.experimental import pallas as pl
from jax.experimental.pallas import tpu as pltpu
from jax.sharding import PartitionSpec as P

MESH = pl.DeviceIdType.MESH
LANES = 128
HALVES = 2


def ranks(live):
    out, rank = [], jnp.int32(0)
    for flag in live:
        out.append(rank)
        rank = rank + flag
    return out


def entry_of_slot(live, rank, slot):
    entry = jnp.int32(0)
    for number, (flag, place) in enumerate(zip(live, rank)):
        entry = entry + jnp.where(jnp.logical_and(flag == 1, place == slot), number, 0)
    return entry


def kernel(
    n_row, n_col,
    e_hbm, l_hbm, ep_hbm, lp_hbm, t_hbm,
    out_ref,
    e_ref, l_ref, t_ref, ep_ref, lp_ref,
    eg_ref, lg_ref, em_ref, lm_ref, cnt_ref, weight_ref, p_ref,
    fetch_sem, count_sem,
    send_e, recv_e, send_own, recv_own, send_far, recv_far, send_core, recv_core,
):
    rows, early_ka, side, _ = e_ref.shape
    cols = l_ref.shape[1]
    slots_e, slots_l = eg_ref.shape[1], lg_ref.shape[1]
    row, col = lax.axis_index("row"), lax.axis_index("col")
    core, chip = lax.rem(row, 2), row // 2
    chips = n_row // 2
    relay = chips == 4
    has_right = col < n_col - 1
    has_left = col > 0

    fetches = [
        pltpu.make_async_copy(src, dst, fetch_sem.at[n])
        for n, (src, dst) in enumerate((
            (ep_hbm, ep_ref), (lp_hbm, lp_ref), (e_hbm, e_ref), (l_hbm, l_ref), (t_hbm, t_ref),
        ))
    ]
    for copy in fetches:
        copy.start()

    partner = (row + 1 - 2 * core, col)
    if relay:
        beside = chip + 1 - 2 * lax.rem(chip, 2)
        across = chip + 2 - 4 * (chip // 2)
        near = core * across + (1 - core) * beside
        other = core * beside + (1 - core) * across
        facing = 3 - chip
        direct = [near, other]
        chip_of = [chip, near, other, facing]
    else:
        direct = [lax.rem(chip + d, chips) for d in range(1, chips)]
        chip_of = [chip] + [lax.rem(chip + chips - d, chips) for d in range(1, chips)]
    to_chip = [(2 * there + core, col) for there in direct]
    messages = len(chip_of)

    barrier = pltpu.get_barrier_semaphore()
    for there, step in ((has_left, -1), (has_right, 1)):
        @pl.when(there)
        def _():
            pl.semaphore_signal(
                barrier, inc=1, device_id=(row, col + step), device_id_type=MESH
            )
    for device in to_chip + [partner]:
        pl.semaphore_signal(barrier, inc=1, device_id=device, device_id_type=MESH)

    fetches[0].wait()
    order = [(a, b) for b in range(early_ka) for a in range(rows)]
    live = [ep_ref[b, a] for a, b in order]
    rank = ranks(live)
    for n, (flag, place) in enumerate(zip(live, rank)):
        em_ref[col, 0, n] = jnp.where(flag == 1, place, slots_e)
    picks_e = [entry_of_slot(live, rank, s) for s in range(slots_e)]
    for s, entry in enumerate(picks_e):
        em_ref[col, 0, len(order) + s] = entry // rows
    fetches[1].wait()
    live = [lp_ref[0, j] for j in range(cols)]
    rank = ranks(live)
    for n, (flag, place) in enumerate(zip(live, rank)):
        lm_ref[row, 0, n] = jnp.where(flag == 1, place, slots_l)
    picks_l = [entry_of_slot(live, rank, s) for s in range(slots_l)]

    def remote(src, dst, send, recv, device):
        return pltpu.make_async_remote_copy(
            src_ref=src, dst_ref=dst, send_sem=send, recv_sem=recv,
            device_id=device, device_id_type=MESH,
        )

    def along(way, hop, chunk):
        step = 1 - 2 * way
        source = col - step * hop
        ref = em_ref.at[source] if chunk == 0 else eg_ref.at[source, chunk - 1]
        return remote(
            ref, ref, send_e.at[way, hop, chunk], recv_e.at[way, hop, chunk], (row, col + step)
        )

    def sends(way, hop):
        if way == 0:
            return jnp.logical_and(has_right, col >= hop)
        return jnp.logical_and(has_left, col + hop < n_col)

    def receives(way, hop):
        return col >= hop + 1 if way == 0 else col + hop + 1 < n_col

    hops = range(n_col - 1)
    chunks = range(slots_e + 1)

    half = slots_l // HALVES

    def later_parts(source, sems):
        send, recv = sems
        parts = [(lm_ref.at[source], send.at[0], recv.at[0])]
        for n in range(HALVES):
            ref = lg_ref.at[source, pl.ds(n * half, half)]
            parts.append((ref, send.at[n + 1], recv.at[n + 1]))
        return parts

    def later(source, sems, device):
        return [remote(ref, ref, s, r, device) for ref, s, r in later_parts(source, sems)]

    fetches[2].wait()
    for s, entry in enumerate(picks_e):
        eg_ref[col, s] = e_ref[lax.rem(entry, rows), entry // rows]
    fetches[3].wait()
    for s, entry in enumerate(picks_l):
        lg_ref[row, s] = l_ref[0, entry]
    ends = has_right.astype(jnp.int32) + has_left.astype(jnp.int32)
    pl.semaphore_wait(barrier, len(to_chip) + 1 + ends)

    def sem_of(pair, n):
        return pair[0].at[n], pair[1].at[n]

    own_out = [
        later(row, sem_of((send_own, recv_own), n), device) for n, device in enumerate(to_chip)
    ]
    core_out = [
        later(2 * there + core, sem_of((send_core, recv_core), n), partner)
        for n, there in enumerate(chip_of)
    ]
    if relay:
        far_out = later(2 * near + core, (send_far, recv_far), to_chip[1])
    for chunk in chunks:
        for way in range(2):
            @pl.when(sends(way, 0))
            def _():
                along(way, 0, chunk).start()
        for group in own_out:
            if chunk <= HALVES:
                group[chunk].start()
    for copy in core_out[0]:
        copy.start()

    for s in range(slots_e + 1):
        p_ref[s, slots_l] = jnp.zeros((side, side), jnp.float32)
    for u in range(slots_l):
        p_ref[slots_e, u] = jnp.zeros((side, side), jnp.float32)
    fetches[4].wait()
    middle = n_row
    lane = lax.broadcasted_iota(jnp.int32, (cols, LANES), 1)
    for i in range(rows):
        numbers = t_ref[i]
        counts = jnp.zeros((cols, LANES), jnp.float32)
        for k in range(middle):
            hits = jnp.sum(jnp.where(numbers == k, 1.0, 0.0), axis=1, keepdims=True)
            counts = jnp.where(lane == k, hits, counts)
        cnt_ref[i * cols:(i + 1) * cols, :] = counts
    to_scalar = pltpu.make_async_copy(cnt_ref, weight_ref, count_sem)
    to_scalar.start()

    def land(hop, chunk):
        for way in range(2):
            @pl.when(receives(way, hop))
            def _():
                along(way, hop, chunk).wait_recv()
            if hop + 1 < n_col - 1:
                @pl.when(sends(way, hop + 1))
                def _():
                    along(way, hop + 1, chunk).start()

    def arrive(message, part):
        if relay:
            if message == 3:
                later(2 * facing + core, (send_far, recv_far), to_chip[1])[part].wait_recv()
            else:
                own_out[message - 1][part].wait_recv()
                if message == 1:
                    far_out[part].start()
        else:
            own_out[message - 1][part].wait_recv()
        core_out[message][part].start()

    early = [(hop, chunk) for hop in hops[:-1] for chunk in chunks]
    rest = [(m, part) for m in range(1, messages) for part in range(HALVES + 1)]
    if relay:
        rest = [(m, part) for part in range(HALVES + 1) for m in (1, 2)]
        rest += [(3, part) for part in range(HALVES + 1)]
    stride = max(1, -(-len(early) // max(1, len(rest))))
    step = 0
    while early or rest:
        if early:
            land(*early.pop(0))
        if rest and step % stride == stride - 1 or not early:
            if rest:
                arrive(*rest.pop(0))
        step += 1
    for group in core_out:
        for copy in group:
            copy.wait_recv()
    to_scalar.wait()

    def form(source, s):
        k = source * early_ka + em_ref[source, 0, len(order) + s]
        wide = jnp.concatenate([lg_ref[k, u] for u in range(slots_l)], axis=1)
        product = jnp.dot(eg_ref[source, s], wide, preferred_element_type=jnp.float32)
        for u in range(slots_l):
            p_ref[s, u] = product[:, u * side:(u + 1) * side]

    def spread(source, fresh):
        def one_row(i, carry):
            for j in range(cols):
                total = None if fresh else out_ref[i, j]
                for b in range(early_ka):
                    k = source * early_ka + b
                    s = em_ref[source, 0, b * rows + i]
                    u = lm_ref[k, 0, j]
                    term = weight_ref[i * cols + j, k] * p_ref[s, u]
                    total = term if total is None else total + term
                out_ref[i, j] = total
            return carry
        lax.fori_loop(0, rows, one_row, 0)

    for s in range(slots_e):
        form(col, s)
    spread(col, True)

    def one_column(source, carry):
        inside = jnp.logical_and(source < col + n_col - 1, source > col - n_col + 1)
        @pl.when(jnp.logical_and(source != col, inside))
        def _():
            for s in range(slots_e):
                form(source, s)
            spread(source, False)
        return carry

    lax.fori_loop(0, n_col, one_column, 0)

    last = n_col - 2
    @pl.when(jnp.logical_or(receives(0, last), receives(1, last)))
    def _():
        source = n_col - 1 - col
        for chunk in chunks:
            land(last, chunk)
            if chunk:
                form(source, chunk - 1)
        spread(source, False)

    for group in own_out + core_out:
        for copy in group:
            copy.wait_send()
    if relay:
        for copy in far_out:
            copy.wait_send()
    for hop in hops:
        for way in range(2):
            @pl.when(sends(way, hop))
            def _():
                for chunk in chunks:
                    along(way, hop, chunk).wait_send()


def on_device(n_row, n_col, earlier_blocks, later_blocks, earlier_pattern, later_pattern, triples):
    rows, early_ka, side, _ = earlier_blocks.shape
    late_kb, cols = later_blocks.shape[:2]
    assert late_kb == 1
    slots_e = max(1, rows * early_ka // 2)
    slots_l = max(1, late_kb * cols // 2)
    chips = n_row // 2
    direct = 2 if chips == 4 else chips - 1
    parts = HALVES + 1
    vmem = pl.BlockSpec(memory_space=pltpu.VMEM)
    hbm = pl.BlockSpec(memory_space=pltpu.HBM)
    block = jnp.bfloat16
    dma = pltpu.SemaphoreType.DMA
    return pl.pallas_call(
        functools.partial(kernel, n_row, n_col),
        out_shape=jax.ShapeDtypeStruct((rows, cols, side, side), jnp.float32),
        in_specs=[hbm] * 5,
        out_specs=vmem,
        scratch_shapes=[
            pltpu.VMEM(earlier_blocks.shape, block),
            pltpu.VMEM(later_blocks.shape, block),
            pltpu.VMEM(triples.shape, jnp.int32),
            pltpu.SMEM((early_ka, rows), jnp.int32),
            pltpu.SMEM(later_pattern.shape, jnp.int32),
            pltpu.VMEM((n_col, slots_e, side, side), block),
            pltpu.VMEM((n_row, slots_l, side, side), block),
            pltpu.SMEM((n_col, 1, LANES), jnp.int32),
            pltpu.SMEM((n_row, 1, LANES), jnp.int32),
            pltpu.VMEM((rows * cols, LANES), jnp.float32),
            pltpu.SMEM((rows * cols, LANES), jnp.float32),
            pltpu.VMEM((slots_e + 1, slots_l + 1, side, side), jnp.float32),
            dma((5,)),
            dma(()),
            dma((2, n_col, slots_e + 1)),
            dma((2, n_col, slots_e + 1)),
            dma((direct, parts)),
            dma((direct, parts)),
            dma((parts,)),
            dma((parts,)),
            dma((chips, parts)),
            dma((chips, parts)),
        ],
        compiler_params=pltpu.CompilerParams(
            collective_id=0, has_side_effects=True, vmem_limit_bytes=32 << 20
        ),
        name="gather_compose",
    )(*(
        pltpu.with_memory_space_constraint(x, pltpu.HBM)
        for x in (earlier_blocks, later_blocks, earlier_pattern.T, later_pattern, triples)
    ))


def solution(mesh):
    return jax.shard_map(
        functools.partial(on_device, mesh.shape["row"], mesh.shape["col"]),
        mesh=mesh,
        in_specs=(
            P("row", "col", None, None),
            P("row", "col", None, None),
            P("row", "col"),
            P("row", "col"),
            P("row", "col", None),
        ),
        out_specs=P("row", "col", None, None),
        check_vma=False,
    )
```

time: 23 us -> 22.4 us (0.974)
  the two profiles are of different devices: /device:TPU:0 before, /device:TPU:1 now
where the time goes in v1:
time: 22.4 us; the launch traced here: 22.2 us
  Pallas kernels  20.9 us (93%)
  local copies, waits for them, and re-layouts  1.32 us (6%)
    pallas_call x1, Pallas kernels, on_device(): pl.pallas_call(functools.partial(kernel, n_row, n_col), out_shape=jax.Sha...  20.9 us
    unnamed x1, local copies, waits for them, and re-layouts  1.32 us

profile of v1, /device:TPU:1, one launch (start us, length us, event | category | flops | bytes accessed | tf_op | source)
XLA Modules:
  0.0 22.2 jit_solution(6935638433969082199)
XLA Ops:
  0.0 20.9 %gather_compose.1 = f32[4,8,128,128]{3,2,1,0:T(8,128)S(1)} custom-call(bf16[4,2,128,128]{3,2,1,0:T(8,128)(2,1)} %e_hbm.1, bf16[1,8,128,128]{3,2,1,0:T(8,128)(2,1)} %l_hbm.1, s32[2,4]{1,0:T(2,128)} %bitcast.1, s32[1,8]{1,0:T(1,128)} %lp_hbm.1, s32[4,8,48]{2,1,0:T(8,128)} %t_hbm.1), custom_call_target="tpu_custom_call" | custom-call | tf_op jit(solution)/shard_map/gather_compose/pallas_call | solution.py:300
  20.9 1.3 %copy.7 = f32[4,8,128,128]{3,2,1,0:T(8,128)} copy(f32[4,8,128,128]{3,2,1,0:T(8,128)S(1)} %gather_compose.1) | data formatting | bytes 4194304

commit v2 on v1

v2 whole, which is shorter than its diff:
```python
import functools

import jax
import jax.numpy as jnp
from jax import lax
from jax.experimental import pallas as pl
from jax.experimental.pallas import tpu as pltpu
from jax.sharding import PartitionSpec as P

MESH = pl.DeviceIdType.MESH
LANES = 128
HALVES = 2


def ranks(live):
    out, rank = [], jnp.int32(0)
    for flag in live:
        out.append(rank)
        rank = rank + flag
    return out


def entry_of_slot(live, rank, slot):
    entry = jnp.int32(0)
    for number, (flag, place) in enumerate(zip(live, rank)):
        entry = entry + jnp.where(jnp.logical_and(flag == 1, place == slot), number, 0)
    return entry


def kernel(
    n_row, n_col,
    e_hbm, l_hbm, ep_hbm, lp_hbm, t_hbm,
    out_ref,
    e_ref, l_ref, t_ref, ep_ref, lp_ref,
    eg_ref, lg_ref, em_ref, lm_ref, cnt_ref, weight_ref, p_ref,
    fetch_sem, count_sem,
    send_e, recv_e, send_on, send_own, recv_own, send_far, recv_far, send_core, recv_core,
):
    rows, early_ka, side, _ = e_ref.shape
    cols = l_ref.shape[1]
    slots_e, slots_l = eg_ref.shape[1], lg_ref.shape[1]
    row, col = lax.axis_index("row"), lax.axis_index("col")
    core, chip = lax.rem(row, 2), row // 2
    chips = n_row // 2
    relay = chips == 4

    fetches = [
        pltpu.make_async_copy(src, dst, fetch_sem.at[n])
        for n, (src, dst) in enumerate((
            (ep_hbm, ep_ref), (lp_hbm, lp_ref), (e_hbm, e_ref), (l_hbm, l_ref), (t_hbm, t_ref),
        ))
    ]
    for copy in fetches:
        copy.start()

    partner = (row + 1 - 2 * core, col)
    if relay:
        beside = chip + 1 - 2 * lax.rem(chip, 2)
        across = chip + 2 - 4 * (chip // 2)
        near = core * across + (1 - core) * beside
        other = core * beside + (1 - core) * across
        facing = 3 - chip
        direct = [near, other]
        chip_of = [chip, near, other, facing]
    else:
        direct = [lax.rem(chip + d, chips) for d in range(1, chips)]
        chip_of = [chip] + [lax.rem(chip + chips - d, chips) for d in range(1, chips)]
    to_chip = [(2 * there + core, col) for there in direct]
    messages = len(chip_of)

    def direct_e(source, target):
        ends = jnp.logical_or(
            jnp.logical_and(target == 0, source >= 2),
            jnp.logical_and(target == n_col - 1, source <= n_col - 3),
        )
        inside = jnp.logical_and(target >= 0, target < n_col)
        return jnp.logical_and(inside, jnp.logical_not(ends))

    def passes(source):
        left = jnp.logical_and(col == 1, source >= 2)
        return jnp.logical_or(left, jnp.logical_and(col == n_col - 2, source <= n_col - 3))

    offsets = [sign * d for d in range(n_col - 1, 0, -1) for sign in (-1, 1)]

    barrier = pltpu.get_barrier_semaphore()
    expected = jnp.int32(len(to_chip) + 1)
    for offset in offsets:
        source = col + offset
        inside = jnp.logical_and(source >= 0, source < n_col)
        @pl.when(jnp.logical_and(inside, direct_e(source, col)))
        def _():
            pl.semaphore_signal(
                barrier, inc=1, device_id=(row, source), device_id_type=MESH
            )
        expected = expected + direct_e(col, source).astype(jnp.int32)
    for device in to_chip + [partner]:
        pl.semaphore_signal(barrier, inc=1, device_id=device, device_id_type=MESH)

    def remote(src, dst, send, recv, device):
        return pltpu.make_async_remote_copy(
            src_ref=src, dst_ref=dst, send_sem=send, recv_sem=recv,
            device_id=device, device_id_type=MESH,
        )

    chunks = range(slots_e + 1)

    def earlier(source, chunk, target, send):
        ref = em_ref.at[source] if chunk == 0 else eg_ref.at[source, chunk - 1]
        return remote(ref, ref, send.at[chunk], recv_e.at[source, chunk], (row, target))

    half = slots_l // HALVES
    parts = range(HALVES + 1)

    def later(source, part, send, recv, device):
        ref = lm_ref.at[source] if part == 0 else lg_ref.at[source, pl.ds((part - 1) * half, half)]
        return remote(ref, ref, send.at[part], recv.at[part], device)

    def own_out(n, part):
        return later(row, part, send_own.at[n], recv_own.at[n], to_chip[n])

    def core_out(n, part):
        return later(2 * chip_of[n] + core, part, send_core.at[n], recv_core.at[n], partner)

    def far_out(part):
        return later(2 * near + core, part, send_far, recv_far, to_chip[1])

    order = [(a, b) for b in range(early_ka) for a in range(rows)]
    fetches[0].wait()
    live = [ep_ref[b, a] for a, b in order]
    rank = ranks(live)
    picks_e = [entry_of_slot(live, rank, s) for s in range(slots_e)]
    for n, (flag, place) in enumerate(zip(live, rank)):
        em_ref[col, 0, n] = jnp.where(flag == 1, place, slots_e)
    for s, entry in enumerate(picks_e):
        em_ref[col, 0, len(order) + s] = entry // rows
    fetches[2].wait()
    for s, entry in enumerate(picks_e):
        eg_ref[col, s] = e_ref[lax.rem(entry, rows), entry // rows]
    pl.semaphore_wait(barrier, expected)
    for offset in offsets:
        target = col + offset
        @pl.when(direct_e(col, target))
        def _():
            for chunk in chunks:
                earlier(col, chunk, target, send_e.at[target]).start()

    fetches[1].wait()
    live = [lp_ref[0, j] for j in range(cols)]
    rank = ranks(live)
    picks_l = [entry_of_slot(live, rank, s) for s in range(slots_l)]
    for n, (flag, place) in enumerate(zip(live, rank)):
        lm_ref[row, 0, n] = jnp.where(flag == 1, place, slots_l)
    fetches[3].wait()
    for s, entry in enumerate(picks_l):
        lg_ref[row, s] = l_ref[0, entry]
    for part in parts:
        for n in range(len(to_chip)):
            own_out(n, part).start()
    for part in parts:
        core_out(0, part).start()

    for s in range(slots_e + 1):
        p_ref[s, slots_l] = jnp.zeros((side, side), jnp.float32)
    for u in range(slots_l):
        p_ref[slots_e, u] = jnp.zeros((side, side), jnp.float32)
    fetches[4].wait()
    middle = n_row
    lane = lax.broadcasted_iota(jnp.int32, (cols, LANES), 1)
    for i in range(rows):
        numbers = t_ref[i]
        counts = jnp.zeros((cols, LANES), jnp.float32)
        for k in range(middle):
            hits = jnp.sum(jnp.where(numbers == k, 1.0, 0.0), axis=1, keepdims=True)
            counts = jnp.where(lane == k, hits, counts)
        cnt_ref[i * cols:(i + 1) * cols, :] = counts
    to_scalar = pltpu.make_async_copy(cnt_ref, weight_ref, count_sem)
    to_scalar.start()

    def await_e(source, chunk):
        earlier(source, chunk, col, send_e.at[source]).wait_recv()

    def hand_on(source, chunk, target):
        await_e(source, chunk)
        earlier(source, chunk, target, send_on.at[source]).start()

    def both_ways(distance, chunk):
        if distance >= n_col - 1:
            return
        @pl.when(col == 1)
        def _():
            hand_on(1 + distance, chunk, 0)
        @pl.when(col == n_col - 2)
        def _():
            hand_on(n_col - 2 - distance, chunk, n_col - 1)

    def arrive(message, part):
        if relay and message == 3:
            later(2 * facing + core, part, send_far, recv_far, to_chip[1]).wait_recv()
        else:
            own_out(message - 1, part).wait_recv()
            if relay and message == 1:
                far_out(part).start()
        core_out(message, part).start()

    if relay:
        arrivals = [(m, part) for part in parts for m in (1, 2)] + [(3, part) for part in parts]
    else:
        arrivals = [(m, part) for m in range(1, messages) for part in parts]
    onward = [(d, chunk) for d in range(1, n_col - 1) for chunk in chunks]
    slots = len(arrivals)
    for n in range(max(len(onward), slots)):
        if n < len(onward):
            both_ways(*onward[n])
        if n < slots:
            arrive(*arrivals[n])
    for n in range(messages):
        for part in parts:
            core_out(n, part).wait_recv()
    to_scalar.wait()

    def form(source, s):
        k = source * early_ka + em_ref[source, 0, len(order) + s]
        wide = jnp.concatenate([lg_ref[k, u] for u in range(slots_l)], axis=1)
        product = jnp.dot(eg_ref[source, s], wide, preferred_element_type=jnp.float32)
        for u in range(slots_l):
            p_ref[s, u] = product[:, u * side:(u + 1) * side]

    def spread(source, fresh):
        def one_row(i, carry):
            for j in range(cols):
                total = None if fresh else out_ref[i, j]
                for b in range(early_ka):
                    k = source * early_ka + b
                    s = em_ref[source, 0, b * rows + i]
                    u = lm_ref[k, 0, j]
                    term = weight_ref[i * cols + j, k] * p_ref[s, u]
                    total = term if total is None else total + term
                out_ref[i, j] = total
            return carry
        lax.fori_loop(0, rows, one_row, 0)

    for s in range(slots_e):
        form(col, s)
    spread(col, True)

    at_end = jnp.logical_or(col == 0, col == n_col - 1)
    last = n_col - 1 - col

    def one_column(number, carry):
        source = jnp.where(col < n_col // 2, number, n_col - 1 - number)
        held_back = jnp.logical_and(at_end, source == last)
        @pl.when(jnp.logical_and(source != col, jnp.logical_not(held_back)))
        def _():
            @pl.when(jnp.logical_not(passes(source)))
            def _():
                for chunk in chunks:
                    await_e(source, chunk)
            for s in range(slots_e):
                form(source, s)
            spread(source, False)
        return carry

    lax.fori_loop(0, n_col, one_column, 0)

    @pl.when(at_end)
    def _():
        for chunk in chunks:
            await_e(last, chunk)
            if chunk:
                form(last, chunk - 1)
        spread(last, False)

    for part in parts:
        for n in range(len(to_chip)):
            own_out(n, part).wait_send()
        for n in range(messages):
            core_out(n, part).wait_send()
        if relay:
            far_out(part).wait_send()
    for offset in offsets:
        target = col + offset
        @pl.when(direct_e(col, target))
        def _():
            for chunk in chunks:
                earlier(col, chunk, target, send_e.at[target]).wait_send()
    for source in range(n_col):
        for end, middle_col in ((0, 1), (n_col - 1, n_col - 2)):
            if abs(source - end) >= 2:
                @pl.when(col == middle_col)
                def _():
                    for chunk in chunks:
                        earlier(source, chunk, end, send_on.at[source]).wait_send()


def on_device(n_row, n_col, earlier_blocks, later_blocks, earlier_pattern, later_pattern, triples):
    rows, early_ka, side, _ = earlier_blocks.shape
    late_kb, cols = later_blocks.shape[:2]
    assert late_kb == 1
    slots_e = max(1, rows * early_ka // 2)
    slots_l = max(1, late_kb * cols // 2)
    chips = n_row // 2
    direct = 2 if chips == 4 else chips - 1
    parts = HALVES + 1
    vmem = pl.BlockSpec(memory_space=pltpu.VMEM)
    hbm = pl.BlockSpec(memory_space=pltpu.HBM)
    block = jnp.bfloat16
    dma = pltpu.SemaphoreType.DMA
    return pl.pallas_call(
        functools.partial(kernel, n_row, n_col),
        out_shape=jax.ShapeDtypeStruct((rows, cols, side, side), jnp.float32),
        in_specs=[hbm] * 5,
        out_specs=vmem,
        scratch_shapes=[
            pltpu.VMEM(earlier_blocks.shape, block),
            pltpu.VMEM(later_blocks.shape, block),
            pltpu.VMEM(triples.shape, jnp.int32),
            pltpu.SMEM((early_ka, rows), jnp.int32),
            pltpu.SMEM(later_pattern.shape, jnp.int32),
            pltpu.VMEM((n_col, slots_e, side, side), block),
            pltpu.VMEM((n_row, slots_l, side, side), block),
            pltpu.SMEM((n_col, 1, LANES), jnp.int32),
            pltpu.SMEM((n_row, 1, LANES), jnp.int32),
            pltpu.VMEM((rows * cols, LANES), jnp.float32),
            pltpu.SMEM((rows * cols, LANES), jnp.float32),
            pltpu.VMEM((slots_e + 1, slots_l + 1, side, side), jnp.float32),
            dma((5,)),
            dma(()),
            dma((n_col, slots_e + 1)),
            dma((n_col, slots_e + 1)),
            dma((n_col, slots_e + 1)),
            dma((direct, parts)),
            dma((direct, parts)),
            dma((parts,)),
            dma((parts,)),
            dma((chips, parts)),
            dma((chips, parts)),
        ],
        compiler_params=pltpu.CompilerParams(
            collective_id=0, has_side_effects=True, vmem_limit_bytes=32 << 20
        ),
        name="gather_compose",
    )(*(
        pltpu.with_memory_space_constraint(x, pltpu.HBM)
        for x in (earlier_blocks, later_blocks, earlier_pattern.T, later_pattern, triples)
    ))


def solution(mesh):
    return jax.shard_map(
        functools.partial(on_device, mesh.shape["row"], mesh.shape["col"]),
        mesh=mesh,
        in_specs=(
            P("row", "col", None, None),
            P("row", "col", None, None),
            P("row", "col"),
            P("row", "col"),
            P("row", "col", None),
        ),
        out_specs=P("row", "col", None, None),
        check_vma=False,
    )
```

time: 22.4 us -> 21 us (0.938)
  the two profiles are of different devices: /device:TPU:1 before, /device:TPU:0 now
where the time goes in v2:
time: 21 us; the launch traced here: 20.9 us
  Pallas kernels  19.5 us (93%)
  local copies, waits for them, and re-layouts  1.32 us (6%)
    pallas_call x1, Pallas kernels, on_device(): pl.pallas_call(functools.partial(kernel, n_row, n_col), out_shape=jax.Sha...  19.5 us
    unnamed x1, local copies, waits for them, and re-layouts  1.32 us

profile of v2, /device:TPU:0, one launch (start us, length us, event | category | flops | bytes accessed | tf_op | source)
XLA Modules:
  0.0 20.9 jit_solution(27459054441656893)
XLA Ops:
  0.0 19.5 %gather_compose.1 = f32[4,8,128,128]{3,2,1,0:T(8,128)S(1)} custom-call(bf16[4,2,128,128]{3,2,1,0:T(8,128)(2,1)} %e_hbm.1, bf16[1,8,128,128]{3,2,1,0:T(8,128)(2,1)} %l_hbm.1, s32[2,4]{1,0:T(2,128)} %bitcast.1, s32[1,8]{1,0:T(1,128)} %lp_hbm.1, s32[4,8,48]{2,1,0:T(8,128)} %t_hbm.1), custom_call_target="tpu_custom_call" | custom-call | tf_op jit(solution)/shard_map/gather_compose/pallas_call | solution.py:308
  19.5 1.3 %copy.7 = f32[4,8,128,128]{3,2,1,0:T(8,128)} copy(f32[4,8,128,128]{3,2,1,0:T(8,128)S(1)} %gather_compose.1) | data formatting | bytes 4194304

commit v3 on v2

--- a/solution.py
+++ b/solution.py
@@ -30,11 +30,11 @@
 def kernel(
     n_row, n_col,
     e_hbm, l_hbm, ep_hbm, lp_hbm, t_hbm,
-    out_ref,
+    out_any,
     e_ref, l_ref, t_ref, ep_ref, lp_ref,
-    eg_ref, lg_ref, em_ref, lm_ref, cnt_ref, weight_ref, p_ref,
+    eg_ref, lg_ref, em_ref, lm_ref, cnt_ref, weight_ref, p_ref, out_ref,
     fetch_sem, count_sem,
-    send_e, recv_e, send_on, send_own, recv_own, send_far, recv_far, send_core, recv_core,
+    send_e, recv_e, send_on, send_own, recv_own, send_core, recv_core, out_sem,
 ):
     rows, early_ka, side, _ = e_ref.shape
     cols = l_ref.shape[1]
@@ -42,7 +42,6 @@
     row, col = lax.axis_index("row"), lax.axis_index("col")
     core, chip = lax.rem(row, 2), row // 2
     chips = n_row // 2
-    relay = chips == 4
 
     fetches = [
         pltpu.make_async_copy(src, dst, fetch_sem.at[n])
@@ -54,14 +53,14 @@
         copy.start()
 
     partner = (row + 1 - 2 * core, col)
-    if relay:
-        beside = chip + 1 - 2 * lax.rem(chip, 2)
-        across = chip + 2 - 4 * (chip // 2)
-        near = core * across + (1 - core) * beside
-        other = core * beside + (1 - core) * across
-        facing = 3 - chip
-        direct = [near, other]
-        chip_of = [chip, near, other, facing]
+    if chips & (chips - 1) == 0:
+        bits = range(chips.bit_length() - 1)
+        steps = sorted(range(1, chips), key=lambda m: (-m.bit_count(), -m))
+        def moved(m):
+            digits = [lax.rem(chip // 2**b, 2) for b in bits]
+            return sum((1 - v if m >> b & 1 else v) * 2**b for b, v in zip(bits, digits))
+        direct = [moved(m) for m in steps]
+        chip_of = [chip] + direct
     else:
         direct = [lax.rem(chip + d, chips) for d in range(1, chips)]
         chip_of = [chip] + [lax.rem(chip + chips - d, chips) for d in range(1, chips)]
@@ -80,7 +79,7 @@
         left = jnp.logical_and(col == 1, source >= 2)
         return jnp.logical_or(left, jnp.logical_and(col == n_col - 2, source <= n_col - 3))
 
-    offsets = [sign * d for d in range(n_col - 1, 0, -1) for sign in (-1, 1)]
+    offsets = [sign * d for d in range(1, n_col) for sign in (-1, 1)]
 
     barrier = pltpu.get_barrier_semaphore()
     expected = jnp.int32(len(to_chip) + 1)
@@ -120,9 +119,6 @@
 
     def core_out(n, part):
         return later(2 * chip_of[n] + core, part, send_core.at[n], recv_core.at[n], partner)
-
-    def far_out(part):
-        return later(2 * near + core, part, send_far, recv_far, to_chip[1])
 
     order = [(a, b) for b in range(early_ka) for a in range(rows)]
     fetches[0].wait()
@@ -153,8 +149,8 @@
     fetches[3].wait()
     for s, entry in enumerate(picks_l):
         lg_ref[row, s] = l_ref[0, entry]
-    for part in parts:
-        for n in range(len(to_chip)):
+    for n in range(len(to_chip)):
+        for part in parts:
             own_out(n, part).start()
     for part in parts:
         core_out(0, part).start()
@@ -194,25 +190,22 @@
             hand_on(n_col - 2 - distance, chunk, n_col - 1)
 
     def arrive(message, part):
-        if relay and message == 3:
-            later(2 * facing + core, part, send_far, recv_far, to_chip[1]).wait_recv()
-        else:
-            own_out(message - 1, part).wait_recv()
-            if relay and message == 1:
-                far_out(part).start()
+        own_out(message - 1, part).wait_recv()
         core_out(message, part).start()
 
-    if relay:
-        arrivals = [(m, part) for part in parts for m in (1, 2)] + [(3, part) for part in parts]
-    else:
-        arrivals = [(m, part) for m in range(1, messages) for part in parts]
-    onward = [(d, chunk) for d in range(1, n_col - 1) for chunk in chunks]
-    slots = len(arrivals)
-    for n in range(max(len(onward), slots)):
-        if n < len(onward):
-            both_ways(*onward[n])
-        if n < slots:
-            arrive(*arrivals[n])
+    nearest = list(range(messages - 1, 0, -1))
+    for chunk in chunks:
+        both_ways(1, chunk)
+    if messages > 2:
+        nearest[:2] = nearest[1::-1]
+    for part in parts:
+        arrive(nearest[0], part)
+    for distance in range(2, n_col - 1):
+        for chunk in chunks:
+            both_ways(distance, chunk)
+    for part in parts:
+        for message in nearest[1:]:
+            arrive(message, part)
     for n in range(messages):
         for part in parts:
             core_out(n, part).wait_recv()
@@ -225,7 +218,10 @@
         for u in range(slots_l):
             p_ref[s, u] = product[:, u * side:(u + 1) * side]
 
-    def spread(source, fresh):
+    def leave(i):
+        return pltpu.make_async_copy(out_ref.at[i], out_any.at[i], out_sem.at[i])
+
+    def spread(source, fresh, final=False):
         def one_row(i, carry):
             for j in range(cols):
                 total = None if fresh else out_ref[i, j]
@@ -236,6 +232,8 @@
                     term = weight_ref[i * cols + j, k] * p_ref[s, u]
                     total = term if total is None else total + term
                 out_ref[i, j] = total
+            if final:
+                leave(i).start()
             return carry
         lax.fori_loop(0, rows, one_row, 0)
 
@@ -268,15 +266,18 @@
             await_e(last, chunk)
             if chunk:
                 form(last, chunk - 1)
-        spread(last, False)
+        spread(last, False, True)
+
+    @pl.when(jnp.logical_not(at_end))
+    def _():
+        for i in range(rows):
+            leave(i).start()
 
     for part in parts:
         for n in range(len(to_chip)):
             own_out(n, part).wait_send()
         for n in range(messages):
             core_out(n, part).wait_send()
-        if relay:
-            far_out(part).wait_send()
     for offset in offsets:
         target = col + offset
         @pl.when(direct_e(col, target))
@@ -290,6 +291,8 @@
                 def _():
                     for chunk in chunks:
                         earlier(source, chunk, end, send_on.at[source]).wait_send()
+    for i in range(rows):
+        leave(i).wait()
 
 
 def on_device(n_row, n_col, earlier_blocks, later_blocks, earlier_pattern, later_pattern, triples):
@@ -299,9 +302,8 @@
     slots_e = max(1, rows * early_ka // 2)
     slots_l = max(1, late_kb * cols // 2)
     chips = n_row // 2
-    direct = 2 if chips == 4 else chips - 1
+    direct = max(1, chips - 1)
     parts = HALVES + 1
-    vmem = pl.BlockSpec(memory_space=pltpu.VMEM)
     hbm = pl.BlockSpec(memory_space=pltpu.HBM)
     block = jnp.bfloat16
     dma = pltpu.SemaphoreType.DMA
@@ -309,7 +311,7 @@
         functools.partial(kernel, n_row, n_col),
         out_shape=jax.ShapeDtypeStruct((rows, cols, side, side), jnp.float32),
         in_specs=[hbm] * 5,
-        out_specs=vmem,
+        out_specs=pl.BlockSpec(memory_space=pl.ANY),
         scratch_shapes=[
             pltpu.VMEM(earlier_blocks.shape, block),
             pltpu.VMEM(later_blocks.shape, block),
@@ -323,6 +325,7 @@
             pltpu.VMEM((rows * cols, LANES), jnp.float32),
             pltpu.SMEM((rows * cols, LANES), jnp.float32),
             pltpu.VMEM((slots_e + 1, slots_l + 1, side, side), jnp.float32),
+            pltpu.VMEM((rows, cols, side, side), jnp.float32),
             dma((5,)),
             dma(()),
             dma((n_col, slots_e + 1)),
@@ -330,10 +333,9 @@
             dma((n_col, slots_e + 1)),
             dma((direct, parts)),
             dma((direct, parts)),
-            dma((parts,)),
-            dma((parts,)),
             dma((chips, parts)),
             dma((chips, parts)),
+            dma((rows,)),
         ],
         compiler_params=pltpu.CompilerParams(
             collective_id=0, has_side_effects=True, vmem_limit_bytes=32 << 20

time: 21 us -> 19.4 us (0.924)
  Pallas kernels: 19.5 us -> 17.9 us
    pallas_call x1, Pallas kernels: 19.5 us -> 17.9 us  [on_device(): pl.pallas_call(functools.partial(kernel, n_row, n_col), out_shape=jax.Sha...]
where the time goes in v3:
time: 19.4 us; the launch traced here: 19.2 us
  Pallas kernels  17.9 us (92%)
  local copies, waits for them, and re-layouts  1.32 us (7%)
    pallas_call x1, Pallas kernels, on_device(): pl.pallas_call(functools.partial(kernel, n_row, n_col), out_shape=jax.Sha...  17.9 us
    unnamed x1, local copies, waits for them, and re-layouts  1.32 us

profile of v3, /device:TPU:0, one launch (start us, length us, event | category | flops | bytes accessed | tf_op | source)
XLA Modules:
  0.0 19.2 jit_solution(13179462515631108483)
XLA Ops:
  0.0 17.9 %gather_compose.1 = f32[4,8,128,128]{3,2,1,0:T(8,128)S(1)} custom-call(bf16[4,2,128,128]{3,2,1,0:T(8,128)(2,1)} %e_hbm.1, bf16[1,8,128,128]{3,2,1,0:T(8,128)(2,1)} %l_hbm.1, s32[2,4]{1,0:T(2,128)} %bitcast.1, s32[1,8]{1,0:T(1,128)} %lp_hbm.1, s32[4,8,48]{2,1,0:T(8,128)} %t_hbm.1), custom_call_target="tpu_custom_call" | custom-call | tf_op jit(solution)/shard_map/gather_compose/pallas_call | solution.py:310
  17.9 1.3 %copy.7 = f32[4,8,128,128]{3,2,1,0:T(8,128)} copy(f32[4,8,128,128]{3,2,1,0:T(8,128)S(1)} %gather_compose.1) | data formatting | bytes 4194304

commit v4 on v2

v4 whole, which is shorter than its diff:
```python
import functools

import jax
import jax.numpy as jnp
from jax import lax
from jax.experimental import pallas as pl
from jax.experimental.pallas import tpu as pltpu
from jax.sharding import PartitionSpec as P

MESH = pl.DeviceIdType.MESH
LANES = 128
HALVES = 2


def ranks(live):
    out, rank = [], jnp.int32(0)
    for flag in live:
        out.append(rank)
        rank = rank + flag
    return out


def entry_of_slot(live, rank, slot):
    entry = jnp.int32(0)
    for number, (flag, place) in enumerate(zip(live, rank)):
        entry = entry + jnp.where(jnp.logical_and(flag == 1, place == slot), number, 0)
    return entry


def kernel(
    n_row, n_col,
    e_hbm, l_hbm, ep_hbm, lp_hbm, t_hbm,
    out_ref,
    e_ref, l_ref, t_ref, ep_ref, lp_ref,
    eg_ref, lg_ref, em_ref, lm_ref, cnt_ref, weight_ref, p_ref,
    fetch_sem, count_sem, ready_sem,
    send_e, recv_e, send_on, send_own, recv_own, send_core, recv_core,
):
    rows, early_ka, side, _ = e_ref.shape
    cols = l_ref.shape[1]
    slots_e, slots_l = eg_ref.shape[1], lg_ref.shape[1]
    row, col = lax.axis_index("row"), lax.axis_index("col")
    core, chip = lax.rem(row, 2), row // 2
    chips = n_row // 2
    bits = range(chips.bit_length() - 1)

    fetches = [
        pltpu.make_async_copy(src, dst, fetch_sem.at[n])
        for n, (src, dst) in enumerate((
            (ep_hbm, ep_ref), (lp_hbm, lp_ref), (e_hbm, e_ref), (l_hbm, l_ref), (t_hbm, t_ref),
        ))
    ]
    for copy in fetches:
        copy.start()

    def digits(number):
        return [lax.rem(number // 2**b, 2) for b in bits]

    def moved(m):
        return sum((1 - v if m >> b & 1 else v) * 2**b for b, v in zip(bits, digits(chip)))

    def apart(there):
        differ = [v + w - 2 * v * w for v, w in zip(digits(chip), digits(there))]
        return sum(v * 2**b for b, v in zip(bits, differ)), sum(differ)

    chip_of = [chip] + [moved(chips - n) for n in range(1, chips)]
    near = [n for n in range(chips - 1, 0, -1) if (chips - n).bit_count() == 1]
    far = [n for n in range(1, chips) if n not in near]
    vouched = chips == 4
    partner = (row + 1 - 2 * core, col)

    def place(n):
        return (2 * chip_of[n] + core, col)

    def direct_e(source, target):
        ends = jnp.logical_or(
            jnp.logical_and(target == 0, source >= 2),
            jnp.logical_and(target == n_col - 1, source <= n_col - 3),
        )
        inside = jnp.logical_and(target >= 0, target < n_col)
        return jnp.logical_and(inside, jnp.logical_not(ends))

    def passes(source):
        left = jnp.logical_and(col == 1, source >= 2)
        return jnp.logical_or(left, jnp.logical_and(col == n_col - 2, source <= n_col - 3))

    offsets = [sign * d for d in range(n_col - 1, 0, -1) for sign in (-1, 1)]

    barrier = pltpu.get_barrier_semaphore()
    greeted = [place(n) for n in (near if vouched else near + far)] + [partner]
    expected = jnp.int32(len(greeted))
    for offset in offsets:
        source = col + offset
        inside = jnp.logical_and(source >= 0, source < n_col)
        @pl.when(jnp.logical_and(inside, direct_e(source, col)))
        def _():
            pl.semaphore_signal(
                barrier, inc=1, device_id=(row, source), device_id_type=MESH
            )
        expected = expected + direct_e(col, source).astype(jnp.int32)
    for device in greeted:
        pl.semaphore_signal(barrier, inc=1, device_id=device, device_id_type=MESH)

    def remote(src, dst, send, recv, device):
        return pltpu.make_async_remote_copy(
            src_ref=src, dst_ref=dst, send_sem=send, recv_sem=recv,
            device_id=device, device_id_type=MESH,
        )

    chunks = range(slots_e + 1)

    def earlier(source, chunk, target, send):
        ref = em_ref.at[source] if chunk == 0 else eg_ref.at[source, chunk - 1]
        return remote(
            ref, ref, send.at[min(chunk, 1)], recv_e.at[source, chunk], (row, target)
        )

    half = slots_l // HALVES
    parts = range(HALVES + 1)

    def later_ref(source, part):
        if part == 0:
            return lm_ref.at[source]
        return lg_ref.at[source, pl.ds((part - 1) * half, half)]

    def own_out(n, part):
        ref = later_ref(row, part)
        return remote(ref, ref, send_own.at[min(part, 1)], recv_own.at[n - 1, part], place(n))

    def core_out(n, part):
        ref = later_ref(2 * chip_of[n] + core, part)
        kind = min(part, 1)
        return remote(ref, ref, send_core.at[kind], recv_core.at[n, kind], partner)

    def drain(ref, sem):
        pltpu.make_async_copy(ref, ref, sem).wait()

    order = [(a, b) for b in range(early_ka) for a in range(rows)]
    fetches[0].wait()
    live = [ep_ref[b, a] for a, b in order]
    rank = ranks(live)
    picks_e = [entry_of_slot(live, rank, s) for s in range(slots_e)]
    for n, (flag, spot) in enumerate(zip(live, rank)):
        em_ref[col, 0, n] = jnp.where(flag == 1, spot, slots_e)
    for s, entry in enumerate(picks_e):
        em_ref[col, 0, len(order) + s] = entry // rows
    fetches[2].wait()
    for s, entry in enumerate(picks_e):
        eg_ref[col, s] = e_ref[lax.rem(entry, rows), entry // rows]
    pl.semaphore_wait(barrier, expected)
    if vouched:
        pl.semaphore_signal(ready_sem, inc=1, device_id=place(near[0]), device_id_type=MESH)
    for offset in offsets:
        target = col + offset
        @pl.when(direct_e(col, target))
        def _():
            for chunk in chunks:
                earlier(col, chunk, target, send_e.at[target]).start()

    fetches[1].wait()
    live = [lp_ref[0, j] for j in range(cols)]
    rank = ranks(live)
    picks_l = [entry_of_slot(live, rank, s) for s in range(slots_l)]
    for n, (flag, spot) in enumerate(zip(live, rank)):
        lm_ref[row, 0, n] = jnp.where(flag == 1, spot, slots_l)
    fetches[3].wait()
    for s, entry in enumerate(picks_l):
        lg_ref[row, s] = l_ref[0, entry]
    for n in near:
        for part in parts:
            own_out(n, part).start()
    for part in parts:
        core_out(0, part).start()
    if vouched:
        pl.semaphore_wait(ready_sem, 1)
    for n in far:
        for part in parts:
            own_out(n, part).start()

    for s in range(slots_e + 1):
        p_ref[s, slots_l] = jnp.zeros((side, side), jnp.float32)
    for u in range(slots_l):
        p_ref[slots_e, u] = jnp.zeros((side, side), jnp.float32)
    fetches[4].wait()
    middle = n_row
    lane = lax.broadcasted_iota(jnp.int32, (cols, LANES), 1)
    for i in range(rows):
        numbers = t_ref[i]
        counts = jnp.zeros((cols, LANES), jnp.float32)
        for k in range(middle):
            hits = jnp.sum(jnp.where(numbers == k, 1.0, 0.0), axis=1, keepdims=True)
            counts = jnp.where(lane == k, hits, counts)
        cnt_ref[i * cols:(i + 1) * cols, :] = counts
    to_scalar = pltpu.make_async_copy(cnt_ref, weight_ref, count_sem)
    to_scalar.start()

    def await_e(source, chunk):
        earlier(source, chunk, col, send_e.at[source]).wait_recv()

    def hand_on(source, chunk, target):
        await_e(source, chunk)
        earlier(source, chunk, target, send_on).start()

    def both_ways(distance, chunk):
        @pl.when(col == 1)
        def _():
            hand_on(1 + distance, chunk, 0)
        @pl.when(col == n_col - 2)
        def _():
            hand_on(n_col - 2 - distance, chunk, n_col - 1)

    onward = [(d, chunk) for d in range(1, n_col - 1) for chunk in chunks]
    for distance, chunk in sorted(onward, key=lambda x: 3 * x[0] + 2 * x[1]):
        both_ways(distance, chunk)

    def arrive(n, part):
        own_out(n, part).wait_recv()
        core_out(n, part).start()

    def form(source, s):
        b = em_ref[source, 0, len(order) + s]
        wide = jnp.concatenate(
            [
                jnp.where(b == 0, lg_ref[2 * source, u], lg_ref[2 * source + 1, u])
                for u in range(slots_l)
            ],
            axis=1,
        )
        product = jnp.dot(eg_ref[source, s], wide, preferred_element_type=jnp.float32)
        for u in range(slots_l):
            p_ref[s, u] = product[:, u * side:(u + 1) * side]

    def spread(source, fresh):
        def one_row(i, carry):
            for j in range(cols):
                total = None if fresh else out_ref[i, j]
                for b in range(early_ka):
                    k = source * early_ka + b
                    s = em_ref[source, 0, b * rows + i]
                    u = lm_ref[k, 0, j]
                    term = weight_ref[i * cols + j, k] * p_ref[s, u]
                    total = term if total is None else total + term
                out_ref[i, j] = total
            return carry
        lax.fori_loop(0, rows, one_row, 0)

    def await_l(source):
        differ, _ = apart(source)
        n = lax.rem(chips - differ, chips)
        k = 2 * source + 1 - core
        for kind, ref in enumerate((lm_ref.at[k], lg_ref.at[k])):
            pltpu.make_async_copy(ref, ref, recv_core.at[n, kind]).wait()

    at_end = jnp.logical_or(col == 0, col == n_col - 1)
    last = n_col - 1 - col

    def all_columns(distant):
        def one_column(number, carry):
            source = jnp.where(col < n_col // 2, number, n_col - 1 - number)
            _, hops = apart(source)
            held_back = jnp.logical_and(at_end, source == last)
            mine = hops > 1 if distant else hops <= 1
            @pl.when(jnp.logical_and(mine, jnp.logical_not(held_back)))
            def _():
                await_l(source)
                @pl.when(jnp.logical_not(jnp.logical_or(source == col, passes(source))))
                def _():
                    for chunk in chunks:
                        await_e(source, chunk)
                for s in range(slots_e):
                    form(source, s)
                spread(source, False)
            return carry
        lax.fori_loop(0, n_col, one_column, 0)

    out_ref[...] = jnp.zeros_like(out_ref)
    for part in parts:
        for n in near:
            arrive(n, part)
    to_scalar.wait()
    all_columns(False)
    for part in parts:
        for n in far:
            arrive(n, part)
    all_columns(True)

    @pl.when(at_end)
    def _():
        await_l(last)
        for chunk in chunks:
            await_e(last, chunk)
            if chunk:
                form(last, chunk - 1)
        spread(last, False)

    drain(lm_ref.at[pl.ds(0, chips - 1)], send_own.at[0])
    drain(lg_ref.at[pl.ds(0, chips - 1)], send_own.at[1])
    drain(lm_ref.at[pl.ds(0, chips)], send_core.at[0])
    drain(lg_ref.at[pl.ds(0, chips)], send_core.at[1])
    for offset in offsets:
        target = col + offset
        @pl.when(direct_e(col, target))
        def _():
            drain(em_ref.at[col], send_e.at[target, 0])
            drain(eg_ref.at[col], send_e.at[target, 1])
    @pl.when(jnp.logical_or(col == 1, col == n_col - 2))
    def _():
        drain(em_ref.at[pl.ds(0, n_col - 2)], send_on.at[0])
        drain(eg_ref.at[pl.ds(0, n_col - 2)], send_on.at[1])


def on_device(n_row, n_col, earlier_blocks, later_blocks, earlier_pattern, later_pattern, triples):
    rows, early_ka, side, _ = earlier_blocks.shape
    late_kb, cols = later_blocks.shape[:2]
    chips = n_row // 2
    assert late_kb == 1 and early_ka == 2 and n_col >= 4
    assert n_row == 2 * chips == 2 * n_col and chips & (chips - 1) == 0
    slots_e = max(1, rows * early_ka // 2)
    slots_l = max(1, late_kb * cols // 2)
    parts = HALVES + 1
    hbm = pl.BlockSpec(memory_space=pltpu.HBM)
    block = jnp.bfloat16
    dma = pltpu.SemaphoreType.DMA
    return pl.pallas_call(
        functools.partial(kernel, n_row, n_col),
        out_shape=jax.ShapeDtypeStruct((rows, cols, side, side), jnp.float32),
        in_specs=[hbm] * 5,
        out_specs=pl.BlockSpec(memory_space=pltpu.VMEM),
        scratch_shapes=[
            pltpu.VMEM(earlier_blocks.shape, block),
            pltpu.VMEM(later_blocks.shape, block),
            pltpu.VMEM(triples.shape, jnp.int32),
            pltpu.SMEM((early_ka, rows), jnp.int32),
            pltpu.SMEM(later_pattern.shape, jnp.int32),
            pltpu.VMEM((n_col, slots_e, side, side), block),
            pltpu.VMEM((n_row, slots_l, side, side), block),
            pltpu.SMEM((n_col, 1, LANES), jnp.int32),
            pltpu.SMEM((n_row, 1, LANES), jnp.int32),
            pltpu.VMEM((rows * cols, LANES), jnp.float32),
            pltpu.SMEM((rows * cols, LANES), jnp.float32),
            pltpu.VMEM((slots_e + 1, slots_l + 1, side, side), jnp.float32),
            dma((5,)),
            dma(()),
            pltpu.SemaphoreType.REGULAR,
            dma((n_col, 2)),
            dma((n_col, slots_e + 1)),
            dma((2,)),
            dma((2,)),
            dma((chips - 1, parts)),
            dma((2,)),
            dma((chips, 2)),
        ],
        compiler_params=pltpu.CompilerParams(
            collective_id=0, has_side_effects=True, vmem_limit_bytes=32 << 20
        ),
        name="gather_compose",
    )(*(
        pltpu.with_memory_space_constraint(x, pltpu.HBM)
        for x in (earlier_blocks, later_blocks, earlier_pattern.T, later_pattern, triples)
    ))


def solution(mesh):
    return jax.shard_map(
        functools.partial(on_device, mesh.shape["row"], mesh.shape["col"]),
        mesh=mesh,
        in_specs=(
            P("row", "col", None, None),
            P("row", "col", None, None),
            P("row", "col"),
            P("row", "col"),
            P("row", "col", None),
        ),
        out_specs=P("row", "col", None, None),
        check_vma=False,
    )
```

time: 21 us -> 20.2 us (0.962)
  the two profiles are of different devices: /device:TPU:0 before, /device:TPU:7 now
where the time goes in v4:
time: 20.2 us; the launch traced here: 20.1 us
  Pallas kernels  18.7 us (93%)
  local copies, waits for them, and re-layouts  1.32 us (7%)
    pallas_call x1, Pallas kernels, on_device(): pl.pallas_call(functools.partial(kernel, n_row, n_col), out_shape=jax.Sha...  18.7 us
    unnamed x1, local copies, waits for them, and re-layouts  1.32 us

profile of v4, /device:TPU:7, one launch (start us, length us, event | category | flops | bytes accessed | tf_op | source)
XLA Modules:
  0.0 20.1 jit_solution(3365379383495391786)
XLA Ops:
  0.0 18.7 %gather_compose.1 = f32[4,8,128,128]{3,2,1,0:T(8,128)S(1)} custom-call(bf16[4,2,128,128]{3,2,1,0:T(8,128)(2,1)} %e_hbm.1, bf16[1,8,128,128]{3,2,1,0:T(8,128)(2,1)} %l_hbm.1, s32[2,4]{1,0:T(2,128)} %bitcast.1, s32[1,8]{1,0:T(1,128)} %lp_hbm.1, s32[4,8,48]{2,1,0:T(8,128)} %t_hbm.1), custom_call_target="tpu_custom_call" | custom-call | tf_op jit(solution)/shard_map/gather_compose/pallas_call | solution.py:324
  18.7 1.3 %copy.7 = f32[4,8,128,128]{3,2,1,0:T(8,128)} copy(f32[4,8,128,128]{3,2,1,0:T(8,128)S(1)} %gather_compose.1) | data formatting | bytes 4194304

commit v5 on v4

--- a/solution.py
+++ b/solution.py
@@ -72,32 +72,22 @@
     def place(n):
         return (2 * chip_of[n] + core, col)
 
-    def direct_e(source, target):
-        ends = jnp.logical_or(
-            jnp.logical_and(target == 0, source >= 2),
-            jnp.logical_and(target == n_col - 1, source <= n_col - 3),
-        )
-        inside = jnp.logical_and(target >= 0, target < n_col)
-        return jnp.logical_and(inside, jnp.logical_not(ends))
-
-    def passes(source):
-        left = jnp.logical_and(col == 1, source >= 2)
-        return jnp.logical_or(left, jnp.logical_and(col == n_col - 2, source <= n_col - 3))
-
-    offsets = [sign * d for d in range(n_col - 1, 0, -1) for sign in (-1, 1)]
+    def on_line(number):
+        return jnp.logical_and(number >= 0, number < n_col)
+
+    toward = jnp.where(col < n_col // 2, 1, -1)
+    at_end = jnp.logical_or(col == 0, col == n_col - 1)
 
     barrier = pltpu.get_barrier_semaphore()
     greeted = [place(n) for n in (near if vouched else near + far)] + [partner]
     expected = jnp.int32(len(greeted))
-    for offset in offsets:
-        source = col + offset
-        inside = jnp.logical_and(source >= 0, source < n_col)
-        @pl.when(jnp.logical_and(inside, direct_e(source, col)))
+    for step in (1, -1):
+        @pl.when(on_line(col + step))
         def _():
             pl.semaphore_signal(
-                barrier, inc=1, device_id=(row, source), device_id_type=MESH
+                barrier, inc=1, device_id=(row, col + step), device_id_type=MESH
             )
-        expected = expected + direct_e(col, source).astype(jnp.int32)
+        expected = expected + on_line(col + step).astype(jnp.int32)
     for device in greeted:
         pl.semaphore_signal(barrier, inc=1, device_id=device, device_id_type=MESH)
 
@@ -150,12 +140,11 @@
     pl.semaphore_wait(barrier, expected)
     if vouched:
         pl.semaphore_signal(ready_sem, inc=1, device_id=place(near[0]), device_id_type=MESH)
-    for offset in offsets:
-        target = col + offset
-        @pl.when(direct_e(col, target))
+    for n, step in enumerate((-1, 1)):
+        @pl.when(on_line(col + step))
         def _():
             for chunk in chunks:
-                earlier(col, chunk, target, send_e.at[target]).start()
+                earlier(col, chunk, col + step, send_e.at[n]).start()
 
     fetches[1].wait()
     live = [lp_ref[0, j] for j in range(cols)]
@@ -171,12 +160,6 @@
             own_out(n, part).start()
     for part in parts:
         core_out(0, part).start()
-    if vouched:
-        pl.semaphore_wait(ready_sem, 1)
-    for n in far:
-        for part in parts:
-            own_out(n, part).start()
-
     for s in range(slots_e + 1):
         p_ref[s, slots_l] = jnp.zeros((side, side), jnp.float32)
     for u in range(slots_l):
@@ -195,23 +178,26 @@
     to_scalar.start()
 
     def await_e(source, chunk):
-        earlier(source, chunk, col, send_e.at[source]).wait_recv()
-
-    def hand_on(source, chunk, target):
-        await_e(source, chunk)
-        earlier(source, chunk, target, send_on).start()
-
-    def both_ways(distance, chunk):
-        @pl.when(col == 1)
+        earlier(source, chunk, col, send_on).wait_recv()
+
+    def hand_on(distance, turn):
+        sign = toward if turn == 0 else -toward
+        source = col + sign * distance
+        @pl.when(jnp.logical_and(on_line(source), on_line(col - sign)))
         def _():
-            hand_on(1 + distance, chunk, 0)
-        @pl.when(col == n_col - 2)
-        def _():
-            hand_on(n_col - 2 - distance, chunk, n_col - 1)
-
-    onward = [(d, chunk) for d in range(1, n_col - 1) for chunk in chunks]
-    for distance, chunk in sorted(onward, key=lambda x: 3 * x[0] + 2 * x[1]):
-        both_ways(distance, chunk)
+            for chunk in chunks:
+                await_e(source, chunk)
+                earlier(source, chunk, col - sign, send_on).start()
+
+    for distance in range(1, n_col - 1):
+        for turn in range(2):
+            hand_on(distance, turn)
+            if distance == 1 and turn == 0:
+                if vouched:
+                    pl.semaphore_wait(ready_sem, 1)
+                for n in far:
+                    for part in parts:
+                        own_out(n, part).start()
 
     def arrive(n, part):
         own_out(n, part).wait_recv()
@@ -251,7 +237,6 @@
         for kind, ref in enumerate((lm_ref.at[k], lg_ref.at[k])):
             pltpu.make_async_copy(ref, ref, recv_core.at[n, kind]).wait()
 
-    at_end = jnp.logical_or(col == 0, col == n_col - 1)
     last = n_col - 1 - col
 
     def all_columns(distant):
@@ -259,11 +244,12 @@
             source = jnp.where(col < n_col // 2, number, n_col - 1 - number)
             _, hops = apart(source)
             held_back = jnp.logical_and(at_end, source == last)
-            mine = hops > 1 if distant else hops <= 1
+            soon = jnp.logical_and(hops <= 1, number < 2)
+            mine = jnp.logical_not(soon) if distant else soon
             @pl.when(jnp.logical_and(mine, jnp.logical_not(held_back)))
             def _():
                 await_l(source)
-                @pl.when(jnp.logical_not(jnp.logical_or(source == col, passes(source))))
+                @pl.when(jnp.logical_and(source != col, at_end))
                 def _():
                     for chunk in chunks:
                         await_e(source, chunk)
@@ -297,16 +283,15 @@
     drain(lg_ref.at[pl.ds(0, chips - 1)], send_own.at[1])
     drain(lm_ref.at[pl.ds(0, chips)], send_core.at[0])
     drain(lg_ref.at[pl.ds(0, chips)], send_core.at[1])
-    for offset in offsets:
-        target = col + offset
-        @pl.when(direct_e(col, target))
+    for n, step in enumerate((-1, 1)):
+        @pl.when(on_line(col + step))
         def _():
-            drain(em_ref.at[col], send_e.at[target, 0])
-            drain(eg_ref.at[col], send_e.at[target, 1])
-    @pl.when(jnp.logical_or(col == 1, col == n_col - 2))
+            drain(em_ref.at[col], send_e.at[n, 0])
+            drain(eg_ref.at[col], send_e.at[n, 1])
+    @pl.when(jnp.logical_not(at_end))
     def _():
-        drain(em_ref.at[pl.ds(0, n_col - 2)], send_on.at[0])
-        drain(eg_ref.at[pl.ds(0, n_col - 2)], send_on.at[1])
+        drain(em_ref.at[pl.ds(0, n_col - 1)], send_on.at[0])
+        drain(eg_ref.at[pl.ds(0, n_col - 1)], send_on.at[1])
 
 
 def on_device(n_row, n_col, earlier_blocks, later_blocks, earlier_pattern, later_pattern, triples):
@@ -342,7 +327,7 @@
             dma((5,)),
             dma(()),
             pltpu.SemaphoreType.REGULAR,
-            dma((n_col, 2)),
+            dma((2, 2)),
             dma((n_col, slots_e + 1)),
             dma((2,)),
             dma((2,)),

time: 20.2 us -> 17.3 us (0.86)
  the two profiles are of different devices: /device:TPU:7 before, /device:TPU:0 now
where the time goes in v5:
time: 17.3 us; the launch traced here: 17.1 us
  Pallas kernels  15.8 us (91%)
  local copies, waits for them, and re-layouts  1.32 us (8%)
    pallas_call x1, Pallas kernels, on_device(): pl.pallas_call(functools.partial(kernel, n_row, n_col), out_shape=jax.Sha...  15.8 us
    unnamed x1, local copies, waits for them, and re-layouts  1.32 us

profile of v5, /device:TPU:0, one launch (start us, length us, event | category | flops | bytes accessed | tf_op | source)
XLA Modules:
  0.0 17.1 jit_solution(5355524190795311322)
XLA Ops:
  0.0 15.8 %gather_compose.1 = f32[4,8,128,128]{3,2,1,0:T(8,128)S(1)} custom-call(bf16[4,2,128,128]{3,2,1,0:T(8,128)(2,1)} %e_hbm.1, bf16[1,8,128,128]{3,2,1,0:T(8,128)(2,1)} %l_hbm.1, s32[2,4]{1,0:T(2,128)} %bitcast.1, s32[1,8]{1,0:T(1,128)} %lp_hbm.1, s32[4,8,48]{2,1,0:T(8,128)} %t_hbm.1), custom_call_target="tpu_custom_call" | custom-call | tf_op jit(solution)/shard_map/gather_compose/pallas_call | solution.py:309
  15.8 1.3 %copy.7 = f32[4,8,128,128]{3,2,1,0:T(8,128)} copy(f32[4,8,128,128]{3,2,1,0:T(8,128)S(1)} %gather_compose.1) | data formatting | bytes 4194304

commit v6 on v5

--- a/solution.py
+++ b/solution.py
@@ -77,6 +77,10 @@
 
     toward = jnp.where(col < n_col // 2, 1, -1)
     at_end = jnp.logical_or(col == 0, col == n_col - 1)
+    skips = n_col == 4
+    leaper = jnp.logical_and(core == 0, col == n_col - 1)
+    skipped = jnp.logical_and(core == 0, col == n_col - 2)
+    landing = jnp.logical_and(core == 0, col == n_col - 3)
 
     barrier = pltpu.get_barrier_semaphore()
     greeted = [place(n) for n in (near if vouched else near + far)] + [partner]
@@ -88,6 +92,13 @@
                 barrier, inc=1, device_id=(row, col + step), device_id_type=MESH
             )
         expected = expected + on_line(col + step).astype(jnp.int32)
+    if skips:
+        @pl.when(landing)
+        def _():
+            pl.semaphore_signal(
+                barrier, inc=1, device_id=(row, col + 2), device_id_type=MESH
+            )
+        expected = expected + leaper.astype(jnp.int32)
     for device in greeted:
         pl.semaphore_signal(barrier, inc=1, device_id=device, device_id_type=MESH)
 
@@ -140,6 +151,11 @@
     pl.semaphore_wait(barrier, expected)
     if vouched:
         pl.semaphore_signal(ready_sem, inc=1, device_id=place(near[0]), device_id_type=MESH)
+    if skips:
+        @pl.when(leaper)
+        def _():
+            for chunk in chunks:
+                earlier(col, chunk, col - 2, send_e.at[1]).start()
     for n, step in enumerate((-1, 1)):
         @pl.when(on_line(col + step))
         def _():
@@ -160,10 +176,12 @@
             own_out(n, part).start()
     for part in parts:
         core_out(0, part).start()
-    for s in range(slots_e + 1):
-        p_ref[s, slots_l] = jnp.zeros((side, side), jnp.float32)
-    for u in range(slots_l):
-        p_ref[slots_e, u] = jnp.zeros((side, side), jnp.float32)
+    out_ref[...] = jnp.zeros_like(out_ref)
+    for at in range(2):
+        for s in range(slots_e + 1):
+            p_ref[at, s, slots_l] = jnp.zeros((side, side), jnp.float32)
+        for u in range(slots_l):
+            p_ref[at, slots_e, u] = jnp.zeros((side, side), jnp.float32)
     fetches[4].wait()
     middle = n_row
     lane = lax.broadcasted_iota(jnp.int32, (cols, LANES), 1)
@@ -177,33 +195,57 @@
     to_scalar = pltpu.make_async_copy(cnt_ref, weight_ref, count_sem)
     to_scalar.start()
 
+    def arrive(n, part):
+        own_out(n, part).wait_recv()
+        core_out(n, part).start()
+
     def await_e(source, chunk):
         earlier(source, chunk, col, send_on).wait_recv()
 
     def hand_on(distance, turn):
         sign = toward if turn == 0 else -toward
         source = col + sign * distance
-        @pl.when(jnp.logical_and(on_line(source), on_line(col - sign)))
+        wanted = jnp.logical_and(on_line(source), on_line(col - sign))
+        if skips:
+            wanted = jnp.logical_and(wanted, jnp.logical_not(landing))
+        @pl.when(wanted)
         def _():
             for chunk in chunks:
                 await_e(source, chunk)
-                earlier(source, chunk, col - sign, send_on).start()
+                if skips and turn == 1 and distance == 1:
+                    @pl.when(jnp.logical_not(skipped))
+                    def _():
+                        earlier(source, chunk, col - sign, send_on).start()
+                else:
+                    earlier(source, chunk, col - sign, send_on).start()
+
+    if vouched:
+        pl.semaphore_wait(ready_sem, 1)
+    for n in far:
+        for part in parts:
+            own_out(n, part).start()
+
+    if skips:
+        @pl.when(landing)
+        def _():
+            both = [(d, chunk) for d in (1, 2) for chunk in chunks]
+            for at, (d, chunk) in enumerate(sorted(both, key=lambda x: 3 * x[0] + 2 * x[1])):
+                await_e(col + d, chunk)
+                earlier(col + d, chunk, col - 1, send_on).start()
+                if at == 1:
+                    for other in chunks:
+                        await_e(col - 1, other)
+                        earlier(col - 1, other, col + 1, send_on).start()
 
     for distance in range(1, n_col - 1):
         for turn in range(2):
             hand_on(distance, turn)
-            if distance == 1 and turn == 0:
-                if vouched:
-                    pl.semaphore_wait(ready_sem, 1)
-                for n in far:
-                    for part in parts:
-                        own_out(n, part).start()
-
-    def arrive(n, part):
-        own_out(n, part).wait_recv()
-        core_out(n, part).start()
-
-    def form(source, s):
+        if distance == 1:
+            for part in parts:
+                for n in near:
+                    arrive(n, part)
+
+    def form(source, s, at=0):
         b = em_ref[source, 0, len(order) + s]
         wide = jnp.concatenate(
             [
@@ -214,18 +256,17 @@
         )
         product = jnp.dot(eg_ref[source, s], wide, preferred_element_type=jnp.float32)
         for u in range(slots_l):
-            p_ref[s, u] = product[:, u * side:(u + 1) * side]
-
-    def spread(source, fresh):
+            p_ref[at, s, u] = product[:, u * side:(u + 1) * side]
+
+    def spread(source, at=0):
         def one_row(i, carry):
             for j in range(cols):
-                total = None if fresh else out_ref[i, j]
+                total = out_ref[i, j]
                 for b in range(early_ka):
                     k = source * early_ka + b
                     s = em_ref[source, 0, b * rows + i]
                     u = lm_ref[k, 0, j]
-                    term = weight_ref[i * cols + j, k] * p_ref[s, u]
-                    total = term if total is None else total + term
+                    total = total + weight_ref[i * cols + j, k] * p_ref[at, s, u]
                 out_ref[i, j] = total
             return carry
         lax.fori_loop(0, rows, one_row, 0)
@@ -238,14 +279,21 @@
             pltpu.make_async_copy(ref, ref, recv_core.at[n, kind]).wait()
 
     last = n_col - 1 - col
+    second = last - toward
 
     def all_columns(distant):
         def one_column(number, carry):
+            late = number >= n_col
+            number = lax.rem(number, n_col)
             source = jnp.where(col < n_col // 2, number, n_col - 1 - number)
             _, hops = apart(source)
-            held_back = jnp.logical_and(at_end, source == last)
-            soon = jnp.logical_and(hops <= 1, number < 2)
-            mine = jnp.logical_not(soon) if distant else soon
+            held_back = jnp.logical_and(
+                at_end, jnp.logical_or(source == last, source == second)
+            )
+            soon = jnp.logical_and(at_end, jnp.logical_and(hops <= 1, number < 2))
+            mine = soon
+            if distant:
+                mine = jnp.logical_and(jnp.logical_not(soon), late == (hops > 1))
             @pl.when(jnp.logical_and(mine, jnp.logical_not(held_back)))
             def _():
                 await_l(source)
@@ -255,14 +303,10 @@
                         await_e(source, chunk)
                 for s in range(slots_e):
                     form(source, s)
-                spread(source, False)
+                spread(source)
             return carry
-        lax.fori_loop(0, n_col, one_column, 0)
-
-    out_ref[...] = jnp.zeros_like(out_ref)
-    for part in parts:
-        for n in near:
-            arrive(n, part)
+        lax.fori_loop(0, 2 * n_col if distant else n_col, one_column, 0)
+
     to_scalar.wait()
     all_columns(False)
     for part in parts:
@@ -272,12 +316,16 @@
 
     @pl.when(at_end)
     def _():
+        await_l(second)
         await_l(last)
-        for chunk in chunks:
-            await_e(last, chunk)
+        both = [(at, chunk) for at in range(2) for chunk in chunks]
+        for at, chunk in sorted(both, key=lambda x: 3 * x[0] + 2 * x[1]):
+            source = (second, last)[at]
+            await_e(source, chunk)
             if chunk:
-                form(last, chunk - 1)
-        spread(last, False)
+                form(source, chunk - 1, at)
+            if chunk == slots_e:
+                spread(source, at)
 
     drain(lm_ref.at[pl.ds(0, chips - 1)], send_own.at[0])
     drain(lg_ref.at[pl.ds(0, chips - 1)], send_own.at[1])
@@ -288,7 +336,19 @@
         def _():
             drain(em_ref.at[col], send_e.at[n, 0])
             drain(eg_ref.at[col], send_e.at[n, 1])
-    @pl.when(jnp.logical_not(at_end))
+    if skips:
+        @pl.when(leaper)
+        def _():
+            drain(em_ref.at[col], send_e.at[1, 0])
+            drain(eg_ref.at[col], send_e.at[1, 1])
+        @pl.when(skipped)
+        def _():
+            drain(em_ref.at[pl.ds(0, n_col - 2)], send_on.at[0])
+            drain(eg_ref.at[pl.ds(0, n_col - 2)], send_on.at[1])
+    full = jnp.logical_not(at_end)
+    if skips:
+        full = jnp.logical_and(full, jnp.logical_not(skipped))
+    @pl.when(full)
     def _():
         drain(em_ref.at[pl.ds(0, n_col - 1)], send_on.at[0])
         drain(eg_ref.at[pl.ds(0, n_col - 1)], send_on.at[1])
@@ -323,7 +383,7 @@
             pltpu.SMEM((n_row, 1, LANES), jnp.int32),
             pltpu.VMEM((rows * cols, LANES), jnp.float32),
             pltpu.SMEM((rows * cols, LANES), jnp.float32),
-            pltpu.VMEM((slots_e + 1, slots_l + 1, side, side), jnp.float32),
+            pltpu.VMEM((2, slots_e + 1, slots_l + 1, side, side), jnp.float32),
             dma((5,)),
             dma(()),
             pltpu.SemaphoreType.REGULAR,

time: 17.3 us -> 17.2 us (level)
  no operation moved by 1% of the time
where the time goes in v6:
time: 17.2 us; the launch traced here: 17 us
  Pallas kernels  15.7 us (91%)
  local copies, waits for them, and re-layouts  1.32 us (8%)
    pallas_call x1, Pallas kernels, on_device(): pl.pallas_call(functools.partial(kernel, n_row, n_col), out_shape=jax.Sha...  15.7 us
    unnamed x1, local copies, waits for them, and re-layouts  1.32 us

profile of v6, /device:TPU:0, one launch (start us, length us, event | category | flops | bytes accessed | tf_op | source)
XLA Modules:
  0.0 17.0 jit_solution(12154492713407577426)
XLA Ops:
  0.0 15.7 %gather_compose.1 = f32[4,8,128,128]{3,2,1,0:T(8,128)S(1)} custom-call(bf16[4,2,128,128]{3,2,1,0:T(8,128)(2,1)} %e_hbm.1, bf16[1,8,128,128]{3,2,1,0:T(8,128)(2,1)} %l_hbm.1, s32[2,4]{1,0:T(2,128)} %bitcast.1, s32[1,8]{1,0:T(1,128)} %lp_hbm.1, s32[4,8,48]{2,1,0:T(8,128)} %t_hbm.1), custom_call_target="tpu_custom_call" | custom-call | tf_op jit(solution)/shard_map/gather_compose/pallas_call | solution.py:369
  15.7 1.3 %copy.7 = f32[4,8,128,128]{3,2,1,0:T(8,128)} copy(f32[4,8,128,128]{3,2,1,0:T(8,128)S(1)} %gather_compose.1) | data formatting | bytes 4194304
